TPU v7x, 32 devices: a whole 2x2x4 slice. The times are simulated.
32 devices in a mesh: section: 4 (over z), seq: 4 (over y, x), tp: 2 (over core).
Axes of the slice: x: 2, y: 2, z: 4, core: 2. Of those that a mesh axis runs over, the one named last changes fastest.
Arguments:
- queries: bfloat16 [4, 1024, 8192], P('section', 'seq', 'tp'), may hold values from -300 to 300
- vision: bfloat16 [128, 7680], P(('section', 'tp'), 'seq'), may hold values from -6 to 6
- kv_weight: bfloat16 [4, 7680, 2048], P('section', 'seq', 'tp'), may hold values from -0.0625 to 0.0625
- key_gain: float32 [4, 128], P('section'), may hold values from 0.25 to 1.75
- head_gate: float32 [4, 64], P('section', 'tp'), may hold values from -1.5 to 1.5
Outputs:
- attended: bfloat16 [4, 1024, 8192], P('section', 'seq', 'tp')
All inputs are finite; a program needn't handle non-finite values.
Results may differ from a plain program's by a relative error of at most 0.01.
The roundings to bfloat16 on the way count: a program that leaves them out, or rounds other values in their place, can miss the bound.
Values may be sent and summed in bfloat16 or wider, within the bound.
A program may use at most 64 MiB of HBM per device.

v0:
```python
import math
import jax
import jax.numpy as jnp
from jax import lax
from jax.sharding import PartitionSpec as P

eps_norm = 1e-05


def normalize(projected, gain, head_dim):
    rows = projected.shape[0]
    shaped = projected.reshape(rows, -1, 2, head_dim)
    keys_raw = shaped[:, :, 0]
    values_raw = shaped[:, :, 1]
    scaled = (
        keys_raw
        * lax.rsqrt(jnp.mean(keys_raw * keys_raw, axis=-1, keepdims=True) + eps_norm)
        * gain
    )
    return (scaled.astype(jnp.bfloat16), values_raw.astype(jnp.bfloat16))


def fold_keys(carry, grouped, keys, values):
    rows = keys.shape[0]
    block = math.gcd(rows, 128)
    key_blocks = keys.reshape(rows // block, block, keys.shape[1], keys.shape[2])
    value_blocks = values.reshape(rows // block, block, values.shape[1], values.shape[2])
    scale = grouped.shape[-1] ** (-0.5)

    def advance(state, blocks):
        running_max, running_sum, weighted = state
        key_block, value_block = blocks
        scores = (
            jnp.einsum("tigd,rid->tigr", grouped, key_block, preferred_element_type=jnp.float32)
            * scale
        )
        new_max = jnp.maximum(running_max, jnp.max(scores, axis=-1))
        factor = jnp.exp(running_max - new_max)
        exp_scores = jnp.exp(scores - new_max[..., None])
        running_sum = running_sum * factor + jnp.sum(exp_scores, axis=-1)
        weighted = weighted * factor[..., None] + jnp.einsum(
            "tigr,rid->tigd",
            exp_scores.astype(jnp.bfloat16),
            value_block,
            preferred_element_type=jnp.float32,
        )
        return ((new_max, running_sum, weighted), None)

    state, unused = lax.scan(advance, carry, (key_blocks, value_blocks))
    return state


def local(queries, vision, kv_weight, key_gain, head_gate):
    local_weight = kv_weight[0]
    head_dim = key_gain.shape[1]
    partials = jnp.dot(
        lax.all_gather(vision, ("section", "tp"), axis=0, tiled=True),
        local_weight,
        preferred_element_type=jnp.float32,
    )
    tokens = queries.shape[1]
    pair_heads = local_weight.shape[1] // (2 * head_dim)
    query_heads = head_gate.shape[1]
    group = query_heads // pair_heads
    grouped = queries[0].reshape(tokens, pair_heads, group, head_dim)
    initial = (
        jnp.full((tokens, pair_heads, group), -1e30, jnp.float32),
        jnp.zeros((tokens, pair_heads, group), jnp.float32),
        jnp.zeros((tokens, pair_heads, group, head_dim), jnp.float32),
    )
    shares = lax.psum_scatter(partials, "seq", scatter_dimension=0, tiled=True)
    keys, values = normalize(shares, key_gain[0], head_dim)
    state = fold_keys(
        initial,
        grouped,
        lax.all_gather(keys, "seq", axis=0, tiled=True),
        lax.all_gather(values, "seq", axis=0, tiled=True),
    )
    running_max, running_sum, weighted = state
    gate = jnp.tanh(head_gate[0]).reshape(1, pair_heads, group, 1)
    result = weighted / running_sum[..., None] * gate
    return result.reshape(1, tokens, query_heads * head_dim).astype(jnp.bfloat16)


def solution(mesh):
    return jax.shard_map(
        local,
        mesh=mesh,
        in_specs=(
            P("section", "seq", "tp"),
            P(("section", "tp"), "seq"),
            P("section", "seq", "tp"),
            P("section", None),
            P("section", "tp"),
        ),
        out_specs=P("section", "seq", "tp"),
        check_vma=False,
    )
```

profile of v0, /device:TPU:0, one launch (start us, length us, event | category | flops | bytes accessed | tf_op | source)
XLA Modules:
  0.0 88.3 jit_solution(7843838622367598786)
XLA Ops:
  6.5 0.0 reduce-scatter.2.cloned.1.call-start
  6.5 16.7 %all_gather.9 = bf16[128,1920]{1,0:T(8,128)(2,1)S(1)} all-gather(bf16[16,1920]{1,0:T(8,128)(2,1)} %param.6), channel_id=1, replica_groups=mesh['section'=4,'seq'=4,'tp'=2] {'section','tp'}, dimensions={0}, use_global_device_ids=true | all-gather | bytes 552960 | tf_op jit(solution)/shard_map/all_gather | solution.py:57
  23.2 0.0 copy-start.2
  23.3 0.0 copy-start.1
  23.3 3.6 %fusion.4 = f32[128,1024]{1,0:T(8,128)} fusion(bf16[128,1920]{1,0:T(8,128)(2,1)S(1)} %all_gather.9, bf16[1,1920,1024]{2,1,0:T(8,128)(2,1)} %param.7), kind=kOutput, calls=%fused_computation.7 | convolution fusion | flops 503316480 | bytes 4947968 | tf_op jit(solution)/shard_map/dot_general | solution.py:56
  26.9 0.0 reduce-scatter.2.cloned.1.call-update
  26.9 2.1 %copy.22 = bf16[32,8,32,128]{3,2,1,0:T(8,128)(2,1)S(1)} copy(bf16[32,8,32,128]{3,1,2,0:T(8,128)(2,1)} %bitcast.48) | data formatting | bytes 4194304
  29.0 0.0 copy-done.2
  29.0 0.1 tanh.11
  29.1 24.1 %reduce-scatter.2.cloned.1.call-done = f32[32,1024]{1,0:T(8,128)} async-done(((f32[128,1024]{1,0:T(8,128)}), f32[32,1024]{1,0:T(8,128)}) %reduce-scatter.2.cloned.1.call-update) | async-done | bytes 131088 | tf_op jit(solution)/shard_map/reduce_scatter | solution.py:71
  53.2 1.0 %reshape.53 = f32[32,4,2,128]{3,2,1,0:T(2,128)S(1)} reshape(f32[32,1024]{1,0:T(8,128)} %reduce-scatter.2.cloned.1.call-done) | data formatting | bytes 262144 | tf_op jit(solution)/shard_map/reshape | solution.py:12
  54.3 0.1 slice.10
  54.4 0.1 multiply_reduce_fusion
  54.5 0.0 copy-done.1
  54.5 0.1 multiply_convert_fusion
  54.6 8.6 %all_gather.10 = bf16[128,4,128]{2,0,1:T(8,128)(2,1)S(1)} all-gather(bf16[32,4,128]{2,0,1:T(8,128)(2,1)S(1)} %multiply_convert_fusion), channel_id=1, replica_groups=mesh['section'=4,'seq'=4,'tp'=2] {'seq'}, dimensions={0}, use_global_device_ids=true | all-gather | bytes 163840 | tf_op jit(solution)/shard_map/all_gather | solution.py:76
  63.2 1.5 %bitcast_reduce_fusion = (f32[256,4,8]{0,2,1:T(8,128)S(1)}, f32[4,128,256,8]{2,1,3,0:T(8,128)S(1)}) fusion(bf16[256,4,8,128]{3,2,1,0:T(8,128)(2,1)S(1)} %bitcast.47, bf16[128,4,128]{2,0,1:T(8,128)(2,1)S(1)} %all_gather.10), kind=kOutput, calls=%fused_computation.5 | convolution fusion | flops 270524416 | bytes 6455296 | tf_op jit(solution)/shard_map/while/body/eval_jaxpr/tigd,rid->tigr/dot_general | solution.py:34
  64.7 0.0 copy-start
  64.7 1.9 %copy-done = f32[4,128,256,8]{2,1,3,0:T(8,128)} copy-done((f32[4,128,256,8]{2,1,3,0:T(8,128)}, f32[4,128,256,8]{2,1,3,0:T(8,128)S(1)}, u32[]{:S(2)}) %copy-start) | copy-done | bytes 4194328
  66.6 0.8 fusion.6
  67.5 7.3 %all-gather = bf16[128,4,1,128]{3,1,2,0:T(4,128)(2,1)S(1)} all-gather(bf16[32,4,1,128]{3,1,2,0:T(4,128)(2,1)S(1)} %copy.31), channel_id=2, replica_groups=mesh['section'=4,'seq'=4,'tp'=2] {'seq'}, dimensions={0}, use_global_device_ids=true | all-gather | bytes 163840 | tf_op jit(solution)/shard_map/all_gather | solution.py:77
  74.8 0.1 copy.14
  75.0 3.6 %fusion.2 = bf16[256,4,8,128]{0,3,2,1:T(8,128)(2,1)S(1)} fusion(f32[4,128,256,8]{2,1,3,0:T(8,128)} %copy-done, f32[4,8]{1,0:T(4,128)S(1)} %tanh.11, f32[256,4,8]{0,2,1:T(8,128)S(1)} %get-tuple-element.18, f32[256,4,8]{0,2,1:T(8,128)S(1)} %broadcast_maximum_fusion, f32[256,4,8]{0,2,1:T(8,128)S(1)} %get-tuple-element.17, bf16[128,4,1,128]{0,3,1,2:T(8,128)(2,1)S(1)} %copy.14), kind=kOutput, calls=%fused_computation.3 | convolution fusion | flops 275775488 | bytes 6520960 | tf_op jit(solution)/shard_map/while/body/eval_jaxpr/tigr,rid->tigd/dot_general | solution.py:41
  78.5 2.9 %copy.16 = bf16[1,256,4096]{2,1,0:T(8,128)(2,1)} copy(bf16[1,256,4096]{1,2,0:T(8,128)(2,1)S(1)} %bitcast.49) | data formatting | bytes 4194304 | tf_op jit(solution)/shard_map/convert_element_type | solution.py:82
  (6 shorter events, 0.1 us)
Async XLA Ops:
  6.5 46.7 %reduce-scatter.2.cloned.1.call-start = ((), (), s32[]{:S(2)}) async-start(), calls=%async_computation.1 | async-start | bytes 655360 | tf_op jit(solution)/shard_map/reduce_scatter | solution.py:71
  23.2 5.8 %copy-start.2 = (f32[1,32]{1,0:T(1,128)S(1)}, f32[1,32]{1,0:T(1,128)}, u32[]{:S(2)}) copy-start(f32[1,32]{1,0:T(1,128)} %param.9) | copy-start | bytes 388
  23.3 31.3 %copy-start.1 = (f32[1,128]{1,0:T(1,128)S(1)}, f32[1,128]{1,0:T(1,128)}, u32[]{:S(2)}) copy-start(f32[1,128]{1,0:T(1,128)} %param.8) | copy-start | bytes 1540
  64.7 1.9 %copy-start = (f32[4,128,256,8]{2,1,3,0:T(8,128)}, f32[4,128,256,8]{2,1,3,0:T(8,128)S(1)}, u32[]{:S(2)}) copy-start(f32[4,128,256,8]{2,1,3,0:T(8,128)S(1)} %get-tuple-element.20) | copy-start | bytes 12582916
Sparse Core Ops, SparseCore 0:
  27.0 26.1 reduce-scatter.1
where the time goes:
time: 88.5 us; the launch traced here: 88.3 us
  blocking collectives  32.6 us (37%)
  waiting for transfers between devices  24.1 us (27%)
  between operations  13.5 us (15%)
  matrix products  8.73 us (10%)
  local copies, waits for them, and re-layouts  8.23 us (9%)
  other arithmetic  1.01 us (1%)
    reduce_scatter x1, waiting for transfers between devices, local(): shares = lax.psum_scatter(partials, 'seq', scatter_dimension=0, tiled=True)  24.1 us
    all_gather x1, blocking collectives, local(): lax.all_gather(vision, ('section', 'tp'), axis=0, tiled=True)  16.7 us
    all_gather x1, blocking collectives, local(): lax.all_gather(keys, 'seq', axis=0, tiled=True)  8.61 us
    all_gather x1, blocking collectives, local(): lax.all_gather(values, 'seq', axis=0, tiled=True)  7.32 us
    unnamed x8, local copies, waits for them, and re-layouts  3.99 us
    dot_general x1, matrix products, local(): jnp.dot(lax.all_gather(vision, ('section', 'tp'), axis=0, tiled=True), lo...  3.65 us
    dot_general x1, matrix products, advance(): jnp.einsum('tigr,rid->tigd', exp_scores.astype(jnp.bfloat16), value_block...  3.58 us
    convert_element_type x1, local copies, waits for them, and re-layouts, local(): result.reshape(1, tokens, query_heads * head_dim).astype(jnp.bfloat16)  2.86 us
  transfers between devices with their start and end apart: 1, of which 1 were waited for; matrix products, arithmetic and copies ran while one was open for 2% of the time, Pallas kernels for 0%

commit v1 on v0

--- a/solution.py
+++ b/solution.py
@@ -1,3 +1,4 @@
+import functools
 import math
 import jax
 import jax.numpy as jnp
@@ -5,6 +6,43 @@
 from jax.sharding import PartitionSpec as P
 
 eps_norm = 1e-05
+
+
+def _lead_scales(xs, dim_i):
+    next_value, y, side_arr = (
+        lax.axis_size(("section", "tp")),
+        lax.axis_index(("section", "tp")),
+        xs.shape[dim_i],
+    )
+    vals = [idx * next_value if dev == dim_i else idx for dev, idx in enumerate(xs.shape)]
+    step_out = lax.dynamic_update_slice_in_dim(
+        jnp.zeros(vals, xs.dtype), xs, y * side_arr, axis=dim_i
+    )
+    piece_out = clean = xs
+    it = 1
+    while it < next_value // 2 + 1:
+        piece_out = lax.ppermute(
+            piece_out,
+            axis_name=("section", "tp"),
+            perm=[(dev, (dev + 1) % next_value) for dev in range(next_value)],
+        )
+        step_out = lax.dynamic_update_slice_in_dim(
+            step_out, piece_out, (y - it) % next_value * side_arr, axis=dim_i
+        )
+        if 2 * it < next_value:
+            clean = lax.ppermute(
+                clean,
+                axis_name=("section", "tp"),
+                perm=[(dev, (dev - 1) % next_value) for dev in range(next_value)],
+            )
+            step_out = lax.dynamic_update_slice_in_dim(
+                step_out, clean, (y + it) % next_value * side_arr, axis=dim_i
+            )
+        it += 1
+    return step_out
+
+
+part_tracks = functools.partial(_lead_scales, dim_i=0)
 
 
 def normalize(projected, gain, head_dim):
@@ -53,11 +91,7 @@
 def local(queries, vision, kv_weight, key_gain, head_gate):
     local_weight = kv_weight[0]
     head_dim = key_gain.shape[1]
-    partials = jnp.dot(
-        lax.all_gather(vision, ("section", "tp"), axis=0, tiled=True),
-        local_weight,
-        preferred_element_type=jnp.float32,
-    )
+    partials = jnp.dot(part_tracks(vision), local_weight, preferred_element_type=jnp.float32)
     tokens = queries.shape[1]
     pair_heads = local_weight.shape[1] // (2 * head_dim)
     query_heads = head_gate.shape[1]

time: 88.5 us -> 93 us (1.051)
  blocking collectives: 32.6 us -> 15.9 us
  starting transfers between devices: 0.01 us -> 11.8 us
  waiting for transfers between devices: 24.1 us -> 32.4 us
  local copies, waits for them, and re-layouts: 8.23 us -> 9.24 us
    all_gather x1 -> x0, blocking collectives: 16.7 us -> none  [local(): lax.all_gather(vision, ('section', 'tp'), axis=0, tiled=True)]
    ppermute x0 -> x7, starting transfers between devices: none -> 11.8 us  [the longest x3 11.3 us: _lead_scales(): lax.ppermute(clean, axis_name=('section', 'tp'), perm=[(dev, (dev - 1) %...]
    ppermute x0 -> x7, waiting for transfers between devices: none -> 10.3 us  [the longest x4 9.58 us: _lead_scales(): lax.ppermute(piece_out, axis_name=('section', 'tp'), perm=[(dev, (dev + 1...]
    reduce_scatter x1, waiting for transfers between devices: 24.1 us -> 22.1 us  [local(): shares = lax.psum_scatter(partials, 'seq', scatter_dimension=0, tiled=True)]
    dynamic_update_slice x0 -> x8, local copies, waits for them, and re-layouts: none -> 0.96 us  [the longest x1 0.87 us: _lead_scales(): lax.dynamic_update_slice_in_dim(jnp.zeros(vals, xs.dtype), xs, y * side_a...]
  transfers between devices with their start and end apart: 1 -> 8, of which waited for: 1 -> 8; matrix products, arithmetic and copies ran while one was open for 2% -> 3% of each run, Pallas kernels for 0% -> 0%
where the time goes in v1:
time: 93 us; the launch traced here: 92.6 us
  waiting for transfers between devices  32.4 us (35%)
  blocking collectives  15.9 us (17%)
  between operations  13.5 us (15%)
  starting transfers between devices  11.8 us (13%)
  local copies, waits for them, and re-layouts  9.24 us (10%)
  matrix products  8.7 us (9%)
  other arithmetic  1.01 us (1%)
    reduce_scatter x1, waiting for transfers between devices, local(): shares = lax.psum_scatter(partials, 'seq', scatter_dimension=0, tiled=True)  22.1 us
    ppermute x3, starting transfers between devices, _lead_scales(): lax.ppermute(clean, axis_name=('section', 'tp'), perm=[(dev, (dev - 1) %...  11.3 us
    ppermute x4, waiting for transfers between devices, _lead_scales(): lax.ppermute(piece_out, axis_name=('section', 'tp'), perm=[(dev, (dev + 1...  9.58 us
    all_gather x1, blocking collectives, local(): lax.all_gather(keys, 'seq', axis=0, tiled=True)  8.61 us
    all_gather x1, blocking collectives, local(): lax.all_gather(values, 'seq', axis=0, tiled=True)  7.32 us
    unnamed x8, local copies, waits for them, and re-layouts  4.01 us
    dot_general x1, matrix products, local(): jnp.dot(part_tracks(vision), local_weight, preferred_element_type=jnp.flo...  3.63 us
    dot_general x1, matrix products, advance(): jnp.einsum('tigr,rid->tigd', exp_scores.astype(jnp.bfloat16), value_block...  3.58 us
  transfers between devices with their start and end apart: 8, of which 8 were waited for; matrix products, arithmetic and copies ran while one was open for 3% of the time, Pallas kernels for 0%

profile of v1, /device:TPU:0, one launch (start us, length us, event | category | flops | bytes accessed | tf_op | source)
XLA Modules:
  0.0 92.6 jit_solution(10795997631212306489)
XLA Ops:
  6.5 0.5 collective-permute-start
  7.0 4.0 %collective-permute-start.1 = (bf16[16,1920]{1,0:T(8,128)(2,1)}, bf16[16,1920]{1,0:T(8,128)(2,1)S(1)}, u32[]{:S(2)}, u32[]{:S(2)}) collective-permute-start(bf16[16,1920]{1,0:T(8,128)(2,1)} %param.6), channel_id=1, source_target_pairs={{0,25},{1,0},{8,1},{9,8},{16,9},{17,16},{24,17},{25,24},{2,27},{3,... | collective-permute-start | bytes 184328 | tf_op jit(solution)/shard_map/ppermute | solution.py:33
  11.1 0.9 constant_dynamic-update-slice_fusion.7
  12.0 1.2 %collective-permute-done = bf16[16,1920]{1,0:T(8,128)(2,1)S(1)} collective-permute-done((bf16[16,1920]{1,0:T(8,128)(2,1)}, bf16[16,1920]{1,0:T(8,128)(2,1)S(1)}, u32[]{:S(2)}, u32[]{:S(2)}) %collective-permute-start) | collective-permute-done | bytes 61472 | tf_op jit(solution)/shard_map/ppermute | solution.py:24
  13.2 3.5 %collective-permute-start.3 = (bf16[16,1920]{1,0:T(8,128)(2,1)S(1)}, bf16[16,1920]{1,0:T(8,128)(2,1)S(1)}, u32[]{:S(2)}, u32[]{:S(2)}) collective-permute-start(bf16[16,1920]{1,0:T(8,128)(2,1)S(1)} %collective-permute-done.1), channel_id=1, source_target_pairs={{0,25},{1,0},{8,1},{9,8},{16,9},{17,16},{24,17},{25,24},{2,27},{3,... | collective-permute-start | bytes 184328 | tf_op jit(solution)/shard_map/ppermute | solution.py:33
  16.7 2.0 %collective-permute-done.2 = bf16[16,1920]{1,0:T(8,128)(2,1)S(1)} collective-permute-done((bf16[16,1920]{1,0:T(8,128)(2,1)S(1)}, bf16[16,1920]{1,0:T(8,128)(2,1)S(1)}, u32[]{:S(2)}, u32[]{:S(2)}) %collective-permute-start.2) | collective-permute-done | bytes 61472 | tf_op jit(solution)/shard_map/ppermute | solution.py:24
  18.7 0.2 collective-permute-done.3
  18.9 3.8 %collective-permute-start.5 = (bf16[16,1920]{1,0:T(8,128)(2,1)S(1)}, bf16[16,1920]{1,0:T(8,128)(2,1)S(1)}, u32[]{:S(2)}, u32[]{:S(2)}) collective-permute-start(bf16[16,1920]{1,0:T(8,128)(2,1)S(1)} %collective-permute-done.3), channel_id=1, source_target_pairs={{0,25},{1,0},{8,1},{9,8},{16,9},{17,16},{24,17},{25,24},{2,27},{3,... | collective-permute-start | bytes 184328 | tf_op jit(solution)/shard_map/ppermute | solution.py:33
  22.8 1.4 %collective-permute-done.4 = bf16[16,1920]{1,0:T(8,128)(2,1)S(1)} collective-permute-done((bf16[16,1920]{1,0:T(8,128)(2,1)S(1)}, bf16[16,1920]{1,0:T(8,128)(2,1)S(1)}, u32[]{:S(2)}, u32[]{:S(2)}) %collective-permute-start.4) | collective-permute-done | bytes 61472 | tf_op jit(solution)/shard_map/ppermute | solution.py:24
  24.2 0.4 collective-permute-done.5
  24.6 5.0 %collective-permute-done.6 = bf16[16,1920]{1,0:T(8,128)(2,1)S(1)} collective-permute-done((bf16[16,1920]{1,0:T(8,128)(2,1)S(1)}, bf16[16,1920]{1,0:T(8,128)(2,1)S(1)}, u32[]{:S(2)}, u32[]{:S(2)}) %collective-permute-start.6) | collective-permute-done | bytes 61472 | tf_op jit(solution)/shard_map/ppermute | solution.py:24
  29.6 3.6 %fusion.4 = f32[128,1024]{1,0:T(8,128)} fusion(bf16[128,1920]{1,0:T(8,128)(2,1)S(1)} %constant_dynamic-update-slice_fusion, bf16[1,1920,1024]{2,1,0:T(8,128)(2,1)} %param.7), kind=kOutput, calls=%fused_computation.7 | convolution fusion | flops 503316480 | bytes 4947968 | tf_op jit(solution)/shard_map/dot_general | solution.py:94
  33.3 2.1 %copy.22 = bf16[32,8,32,128]{3,2,1,0:T(8,128)(2,1)S(1)} copy(bf16[32,8,32,128]{3,1,2,0:T(8,128)(2,1)} %bitcast.48) | data formatting | bytes 4194304
  35.5 22.1 %reduce-scatter.2.cloned.1.call-done = f32[32,1024]{1,0:T(8,128)} async-done(((f32[128,1024]{1,0:T(8,128)}), f32[32,1024]{1,0:T(8,128)}) %reduce-scatter.2.cloned.1.call-update) | async-done | bytes 131088 | tf_op jit(solution)/shard_map/reduce_scatter | solution.py:105
  57.6 1.0 %reshape.53 = f32[32,4,2,128]{3,2,1,0:T(2,128)S(1)} reshape(f32[32,1024]{1,0:T(8,128)} %reduce-scatter.2.cloned.1.call-done) | data formatting | bytes 262144 | tf_op jit(solution)/shard_map/reshape | solution.py:50
  58.8 0.1 multiply_reduce_fusion
  59.0 8.6 %all_gather.6 = bf16[128,4,128]{2,0,1:T(8,128)(2,1)S(1)} all-gather(bf16[32,4,128]{2,0,1:T(8,128)(2,1)S(1)} %multiply_convert_fusion), channel_id=1, replica_groups=mesh['section'=4,'seq'=4,'tp'=2] {'seq'}, dimensions={0}, use_global_device_ids=true | all-gather | bytes 163840 | tf_op jit(solution)/shard_map/all_gather | solution.py:110
  67.6 1.5 %bitcast_reduce_fusion = (f32[256,4,8]{0,2,1:T(8,128)S(1)}, f32[4,128,256,8]{2,1,3,0:T(8,128)S(1)}) fusion(bf16[256,4,8,128]{3,2,1,0:T(8,128)(2,1)S(1)} %bitcast.47, bf16[128,4,128]{2,0,1:T(8,128)(2,1)S(1)} %all_gather.6), kind=kOutput, calls=%fused_computation.5 | convolution fusion | flops 270524416 | bytes 6455296 | tf_op jit(solution)/shard_map/while/body/eval_jaxpr/tigd,rid->tigr/dot_general | solution.py:72
  69.1 1.9 %copy-done = f32[4,128,256,8]{2,1,3,0:T(8,128)} copy-done((f32[4,128,256,8]{2,1,3,0:T(8,128)}, f32[4,128,256,8]{2,1,3,0:T(8,128)S(1)}, u32[]{:S(2)}) %copy-start) | copy-done | bytes 4194328
  71.0 0.8 fusion.6
  71.9 7.3 %all-gather = bf16[128,4,1,128]{3,1,2,0:T(4,128)(2,1)S(1)} all-gather(bf16[32,4,1,128]{3,1,2,0:T(4,128)(2,1)S(1)} %copy.31), channel_id=2, replica_groups=mesh['section'=4,'seq'=4,'tp'=2] {'seq'}, dimensions={0}, use_global_device_ids=true | all-gather | bytes 163840 | tf_op jit(solution)/shard_map/all_gather | solution.py:111
  79.2 0.1 copy.14
  79.4 3.6 %fusion.2 = bf16[256,4,8,128]{0,3,2,1:T(8,128)(2,1)S(1)} fusion(f32[4,128,256,8]{2,1,3,0:T(8,128)} %copy-done, f32[4,8]{1,0:T(4,128)S(1)} %tanh.11, f32[256,4,8]{0,2,1:T(8,128)S(1)} %get-tuple-element.18, f32[256,4,8]{0,2,1:T(8,128)S(1)} %broadcast_maximum_fusion, f32[256,4,8]{0,2,1:T(8,128)S(1)} %get-tuple-element.17, bf16[128,4,1,128]{0,3,1,2:T(8,128)(2,1)S(1)} %copy.14), kind=kOutput, calls=%fused_computation.3 | convolution fusion | flops 275775488 | bytes 6520960 | tf_op jit(solution)/shard_map/while/body/eval_jaxpr/tigr,rid->tigd/dot_general | solution.py:79
  82.9 2.9 %copy.16 = bf16[1,256,4096]{2,1,0:T(8,128)(2,1)} copy(bf16[1,256,4096]{1,2,0:T(8,128)(2,1)S(1)} %bitcast.49) | data formatting | bytes 4194304 | tf_op jit(solution)/shard_map/convert_element_type | solution.py:116
  (28 shorter events, 0.6 us)
Async XLA Ops:
  6.5 51.1 %reduce-scatter.2.cloned.1.call-start = ((), (), s32[]{:S(2)}) async-start(), calls=%async_computation.1 | async-start | bytes 655360 | tf_op jit(solution)/shard_map/reduce_scatter | solution.py:105
  6.5 6.6 %collective-permute-start = (bf16[16,1920]{1,0:T(8,128)(2,1)}, bf16[16,1920]{1,0:T(8,128)(2,1)S(1)}, u32[]{:S(2)}, u32[]{:S(2)}) collective-permute-start(bf16[16,1920]{1,0:T(8,128)(2,1)} %param.6), channel_id=1, source_target_pairs={{0,1},{1,8},{8,9},{9,16},{16,17},{17,24},{24,25},{25,0},{2,3},{3,1... | collective-permute-start | bytes 184328 | tf_op jit(solution)/shard_map/ppermute | solution.py:24
  7.0 6.2 %collective-permute-start.1 = (bf16[16,1920]{1,0:T(8,128)(2,1)}, bf16[16,1920]{1,0:T(8,128)(2,1)S(1)}, u32[]{:S(2)}, u32[]{:S(2)}) collective-permute-start(bf16[16,1920]{1,0:T(8,128)(2,1)} %param.6), channel_id=1, source_target_pairs={{0,25},{1,0},{8,1},{9,8},{16,9},{17,16},{24,17},{25,24},{2,27},{3,... | collective-permute-start | bytes 184328 | tf_op jit(solution)/shard_map/ppermute | solution.py:33
  13.2 5.5 %collective-permute-start.2 = (bf16[16,1920]{1,0:T(8,128)(2,1)S(1)}, bf16[16,1920]{1,0:T(8,128)(2,1)S(1)}, u32[]{:S(2)}, u32[]{:S(2)}) collective-permute-start(bf16[16,1920]{1,0:T(8,128)(2,1)S(1)} %collective-permute-done), channel_id=1, source_target_pairs={{0,1},{1,8},{8,9},{9,16},{16,17},{17,24},{24,25},{25,0},{2,3},{3,1... | collective-permute-start | bytes 184328 | tf_op jit(solution)/shard_map/ppermute | solution.py:24
  13.2 5.7 %collective-permute-start.3 = (bf16[16,1920]{1,0:T(8,128)(2,1)S(1)}, bf16[16,1920]{1,0:T(8,128)(2,1)S(1)}, u32[]{:S(2)}, u32[]{:S(2)}) collective-permute-start(bf16[16,1920]{1,0:T(8,128)(2,1)S(1)} %collective-permute-done.1), channel_id=1, source_target_pairs={{0,25},{1,0},{8,1},{9,8},{16,9},{17,16},{24,17},{25,24},{2,27},{3,... | collective-permute-start | bytes 184328 | tf_op jit(solution)/shard_map/ppermute | solution.py:33
  18.7 5.4 %collective-permute-start.4 = (bf16[16,1920]{1,0:T(8,128)(2,1)S(1)}, bf16[16,1920]{1,0:T(8,128)(2,1)S(1)}, u32[]{:S(2)}, u32[]{:S(2)}) collective-permute-start(bf16[16,1920]{1,0:T(8,128)(2,1)S(1)} %collective-permute-done.2), channel_id=1, source_target_pairs={{0,1},{1,8},{8,9},{9,16},{16,17},{17,24},{24,25},{25,0},{2,3},{3,1... | collective-permute-start | bytes 184328 | tf_op jit(solution)/shard_map/ppermute | solution.py:24
  18.9 5.7 %collective-permute-start.5 = (bf16[16,1920]{1,0:T(8,128)(2,1)S(1)}, bf16[16,1920]{1,0:T(8,128)(2,1)S(1)}, u32[]{:S(2)}, u32[]{:S(2)}) collective-permute-start(bf16[16,1920]{1,0:T(8,128)(2,1)S(1)} %collective-permute-done.3), channel_id=1, source_target_pairs={{0,25},{1,0},{8,1},{9,8},{16,9},{17,16},{24,17},{25,24},{2,27},{3,... | collective-permute-start | bytes 184328 | tf_op jit(solution)/shard_map/ppermute | solution.py:33
  24.2 5.4 %collective-permute-start.6 = (bf16[16,1920]{1,0:T(8,128)(2,1)S(1)}, bf16[16,1920]{1,0:T(8,128)(2,1)S(1)}, u32[]{:S(2)}, u32[]{:S(2)}) collective-permute-start(bf16[16,1920]{1,0:T(8,128)(2,1)S(1)} %collective-permute-done.4), channel_id=1, source_target_pairs={{0,1},{1,8},{8,9},{9,16},{16,17},{17,24},{24,25},{25,0},{2,3},{3,1... | collective-permute-start | bytes 184328 | tf_op jit(solution)/shard_map/ppermute | solution.py:24
  29.6 5.8 %copy-start.2 = (f32[1,32]{1,0:T(1,128)S(1)}, f32[1,32]{1,0:T(1,128)}, u32[]{:S(2)}) copy-start(f32[1,32]{1,0:T(1,128)} %param.9) | copy-start | bytes 388
  29.6 29.3 %copy-start.1 = (f32[1,128]{1,0:T(1,128)S(1)}, f32[1,128]{1,0:T(1,128)}, u32[]{:S(2)}) copy-start(f32[1,128]{1,0:T(1,128)} %param.8) | copy-start | bytes 1540
  69.1 1.9 %copy-start = (f32[4,128,256,8]{2,1,3,0:T(8,128)}, f32[4,128,256,8]{2,1,3,0:T(8,128)S(1)}, u32[]{:S(2)}) copy-start(f32[4,128,256,8]{2,1,3,0:T(8,128)S(1)} %get-tuple-element.20) | copy-start | bytes 12582916
Sparse Core Ops, SparseCore 0:
  33.4 24.1 reduce-scatter.1
